TPU v7x, 32 devices: a whole 2x2x4 slice. The times are simulated.
32 devices in a mesh: seq: 4 (over y, x), tp: 8 (over z, core).
Axes of the slice: x: 2, y: 2, z: 4, core: 2. Of those that a mesh axis runs over, the one named last changes fastest.
Arguments:
- tokens: bfloat16 [2048, 2560], P('seq'), may hold values from -6 to 6
- expert_ids: int32 [2048, 6], P('seq'), may hold values from 0 to 15, all different within a row; in each aligned block of 512 rows (0 to 511, 512 to 1023, ...) at most 288 rows name the same one
- gate_weights: bfloat16 [2048, 6], P('seq'), may hold values from 0.049804688 to 0.34960938
- live: int32 [2048], P('seq'), may hold values 0 or 1
- norm_gain: float32 [2560], replicated, may hold values from 0.5 to 1.5
- expert_gate: bfloat16 [16, 1536, 2560], P('tp', 'seq'), may hold values from -0.125 to 0.125
- expert_up: bfloat16 [16, 1536, 2560], P('tp', 'seq'), may hold values from -0.125 to 0.125
- expert_down: bfloat16 [16, 1536, 2560], P('tp', 'seq'), may hold values from -0.15625 to 0.15625
- shared_gate: bfloat16 [1536, 2560], P('seq'), may hold values from -0.125 to 0.125
- shared_up: bfloat16 [1536, 2560], P('seq'), may hold values from -0.125 to 0.125
- shared_down: bfloat16 [1536, 2560], P('seq'), may hold values from -0.15625 to 0.15625
Outputs:
- mixed: bfloat16 [2048, 2560], P(('seq', 'tp'))
Inputs may be any that keep to these rules, and one draw needn't show every extreme that they name: `expert_ids`: each row names 6 different experts. In each aligned block of 512 rows (the tokens of one index of seq) no expert is named by more than 288 rows, a bound that some block reaches.
All inputs are finite; a program needn't handle non-finite values. No bound on the sum of `live` on one device may be relied on, other than what follows from the above.
Results may differ from a plain program's by a relative error of at most 0.017.
Values may be sent and summed in bfloat16 or wider, within the bound.
A program may use at most 128 MiB of HBM per device.

v0:
```python
from functools import partial

import jax
import jax.numpy as jnp
from jax import lax
from jax.sharding import PartitionSpec as P


def rms_rows(tokens, norm_gain):
    values = tokens.astype(jnp.float32)
    scale = lax.rsqrt(jnp.mean(values * values, axis=-1, keepdims=True) + 1e-05)
    return (values * scale * norm_gain).astype(jnp.bfloat16)


def place_slots(ids_block, weight_block, first_expert, columns, capacity):
    row_count = ids_block.shape[0]
    owned_ids = first_expert + jnp.arange(columns, dtype=jnp.int32)
    matches = ids_block[:, :, None] == owned_ids[None, None, :]
    matched = jnp.any(matches, axis=1)
    weight = jnp.sum(jnp.where(matches, weight_block[:, :, None], 0.0), axis=1)
    position = jnp.cumsum(matched.astype(jnp.int32), axis=0) - 1
    slot_pos = jnp.where(matched, position, capacity)
    column_index = jnp.broadcast_to(jnp.arange(columns, dtype=jnp.int32)[None, :], slot_pos.shape)
    token_index = jnp.broadcast_to(jnp.arange(row_count, dtype=jnp.int32)[:, None], slot_pos.shape)
    slot_token = (
        jnp.full((capacity, columns), row_count, jnp.int32)
        .at[slot_pos, column_index]
        .set(token_index, mode="drop")
    )
    slot_weight = (
        jnp.zeros((capacity, columns), jnp.float32)
        .at[slot_pos, column_index]
        .set(weight, mode="drop")
    )
    return (slot_token, slot_weight)


def pick_rows(normed_block, slot_token):
    row_count = normed_block.shape[0]
    valid = slot_token < row_count
    picked = jnp.take(normed_block, jnp.minimum(slot_token, row_count - 1), axis=0)
    return jnp.where(valid[..., None], picked, jnp.zeros((), jnp.bfloat16))


def on_device(
    tokens,
    expert_ids,
    gate_weights,
    live,
    norm_gain,
    expert_gate,
    expert_up,
    expert_down,
    shared_gate,
    shared_up,
    shared_down,
):
    tok_seq = tokens.shape[0]
    width = tokens.shape[1]
    top_k = expert_ids.shape[1]
    columns = expert_gate.shape[0]
    n_seq = lax.axis_size("seq")
    n_tp = lax.axis_size("tp")
    capacity = tok_seq * top_k * 3 // (columns * n_tp * 2)
    tok_dev = tok_seq // n_tp
    first_expert = lax.axis_index("tp") * columns
    share_start = lax.axis_index("tp") * tok_dev
    normed = rms_rows(tokens, norm_gain)
    weight_eff = gate_weights * live[:, None].astype(jnp.bfloat16)
    own_token, own_weight = place_slots(
        expert_ids, weight_eff.astype(jnp.float32), first_expert, columns, capacity
    )
    all_rows, all_ids, all_weights = (
        lax.all_gather(normed, "seq", axis=0, tiled=True),
        lax.all_gather(expert_ids.astype(jnp.bfloat16), "seq", axis=0, tiled=True),
        lax.all_gather(weight_eff, "seq", axis=0, tiled=True),
    )
    block_rows = all_rows.reshape(n_seq, tok_seq, width)
    block_ids = all_ids.astype(jnp.int32).reshape(n_seq, tok_seq, top_k)
    block_weights = all_weights.astype(jnp.float32).reshape(n_seq, tok_seq, top_k)
    placer = partial(place_slots, first_expert=first_expert, columns=columns, capacity=capacity)
    slot_tokens, block_slot_weights = jax.vmap(placer)(block_ids, block_weights)
    routed_rows = jax.vmap(pick_rows)(block_rows, slot_tokens).reshape(
        n_seq * capacity, columns, width
    )
    shared_rows = lax.dynamic_slice_in_dim(block_rows, share_start, tok_dev, 1).reshape(
        n_seq * tok_dev, width
    )
    piece = routed_rows
    gate_part = jnp.einsum("cjd,jhd->cjh", piece, expert_gate, preferred_element_type=jnp.float32)
    up_part = jnp.einsum("cjd,jhd->cjh", piece, expert_up, preferred_element_type=jnp.float32)
    hidden = (jax.nn.silu(gate_part) * up_part).astype(jnp.bfloat16)
    expert_out = lax.psum_scatter(
        jnp.einsum("cjh,jhd->cjd", hidden, expert_down, preferred_element_type=jnp.float32).astype(
            jnp.bfloat16
        ),
        "seq",
        scatter_dimension=0,
        tiled=True,
    ).astype(jnp.float32)
    piece = shared_rows
    gate_part = jnp.einsum("rd,hd->rh", piece, shared_gate, preferred_element_type=jnp.float32)
    up_part = jnp.einsum("rd,hd->rh", piece, shared_up, preferred_element_type=jnp.float32)
    hidden = (jax.nn.silu(gate_part) * up_part).astype(jnp.bfloat16)
    shared_out = lax.psum_scatter(
        jnp.dot(hidden, shared_down, preferred_element_type=jnp.float32).astype(jnp.bfloat16),
        "seq",
        scatter_dimension=0,
        tiled=True,
    ).astype(jnp.float32)
    weighted = (expert_out * own_weight[:, :, None]).reshape(capacity * columns, width)
    routed_local = (
        jnp.zeros((tok_seq, width), jnp.float32)
        .at[own_token.reshape(-1)]
        .add(weighted, mode="drop")
    )
    routed = lax.psum_scatter(
        routed_local.astype(jnp.bfloat16), "tp", scatter_dimension=0, tiled=True
    ).astype(jnp.float32)
    return (routed + shared_out).astype(jnp.bfloat16)


def solution(mesh):
    placed = (
        P("seq", None),
        P("seq", None),
        P("seq", None),
        P("seq"),
        P(),
        P("tp", "seq", None),
        P("tp", "seq", None),
        P("tp", "seq", None),
        P("seq", None),
        P("seq", None),
        P("seq", None),
    )
    return jax.shard_map(
        on_device, mesh=mesh, in_specs=placed, out_specs=P(("seq", "tp"), None), check_vma=False
    )
```

profile of v0, /device:TPU:0, one launch (start us, length us, event | category | flops | bytes accessed | tf_op | source)
XLA Modules:
  0.0 479.8 jit_solution(1701159155771079637)
XLA Ops:
  6.5 2.5 fusion.10
  9.0 0.2 copy-done.1
  9.2 2.9 fusion.12
  12.1 0.0 all-gather.2.cloned.1.call-update
  12.2 0.0 reduce-scatter.4.cloned.1.call-start
  12.2 9.6 %all_gather.6 = bf16[2048,6]{0,1:T(8,128)(2,1)S(1)} all-gather(bf16[512,6]{0,1:T(8,128)(2,1)S(1)} %convert_element_type.58), channel_id=1, replica_groups=mesh['seq'=4,'tp'=8] {'seq'}, dimensions={0}, use_global_device_ids=true | all-gather | bytes 30720 | tf_op jit(solution)/shard_map/all_gather | solution.py:75
  21.9 0.1 compare_reduce_fusion
  22.1 2.4 reduce-window.16
  24.5 0.3 slice_reduce_fusion
  24.8 0.7 reduce-window.19
  25.5 0.1 add_add_fusion
  25.7 0.1 multiply_reduce_fusion
  25.8 0.1 and_reduce_fusion
  25.9 0.4 copy.49
  26.3 0.5 reshape.158
  26.7 0.1 broadcast_in_dim.111
  26.8 0.5 reshape.160
  27.3 15.7 %scatter_custom_fusion.2 = s32[2304]{0:T(1024)S(1)} fusion(s32[4096]{0:T(1024)S(1)} %reshape.158, s32[4096]{0:T(1024)S(1)} %reshape.160, s32[]{:T(128)} %constant.18.clone.1), kind=kCustom, calls=%fused_computation.63 | custom fusion | bytes 9220
  43.0 0.1 reshape.137
  43.1 0.1 reshape.135
  43.2 0.1 broadcast_in_dim.112
  43.3 0.1 broadcast_in_dim.114
  43.5 0.2 copy.52
  43.7 0.3 reshape.138
  44.0 76.0 %all-gather.2.cloned.1.call-done = bf16[2048,2560]{1,0:T(8,128)(2,1)} async-done(((bf16[512,2560]{1,0:T(8,128)(2,1)}), bf16[2048,2560]{1,0:T(8,128)(2,1)}) %all-gather.2.cloned.1.call-update) | async-done | bytes 10485776 | tf_op jit(solution)/shard_map/all_gather | solution.py:74
  120.1 74.8 %gather_fusion = bf16[2304,2560]{1,0:T(8,128)(2,1)} fusion(bf16[4,512,2560]{2,1,0:T(8,128)(2,1)} %bitcast.76, s32[2304]{0:T(1024)S(1)} %reshape.138), kind=kCustom, calls=%fused_computation | custom fusion | bytes 23611392 | tf_op jit(solution)/shard_map/vmap(jit(_take))/gather | solution.py:41
  194.9 23.5 %gather.7 = bf16[1152,2,2560]{2,1,0:T(2,128)(2,1)} reshape(bf16[2304,2560]{1,0:T(8,128)(2,1)} %gather_fusion) | data formatting | bytes 23592960 | tf_op jit(solution)/shard_map/vmap(jit(_take))/gather | solution.py:41
  218.4 12.8 %fusion.13 = f32[1152,2,384]{2,0,1:T(8,128)} fusion(bf16[2,384,2560]{2,1,0:T(8,128)(2,1)} %param.16, bf16[1152,2,2560]{2,1,0:T(2,128)(2,1)} %gather.7, pred[1152,2]{0,1:T(4,128)(4,1)S(1)} %broadcast_in_dim.114, pred[1152,2]{0,1:T(4,128)(4,1)S(1)} %broadcast_in_dim.112), kind=kOutput, calls=%fused_computation.22 | convolution fusion | flops 4541644800 | bytes 19272192 | tf_op jit(solution)/shard_map/cjd,jhd->cjh/dot_general | solution.py:90
  231.3 21.3 %fusion = bf16[1152,2,2560]{2,0,1:T(8,128)(2,1)} fusion(bf16[2,384,2560]{2,1,0:T(8,128)(2,1)} %param.18, bf16[2,384,2560]{2,1,0:T(8,128)(2,1)} %param.17, bf16[1152,2,2560]{2,1,0:T(2,128)(2,1)} %gather.7, pred[1152,2]{0,1:T(4,128)(4,1)S(1)} %broadcast_in_dim.114, pred[1152,2]{0,1:T(4,128)(4,1)S(1)} %broadcast_in_dim.112, f32[1152,2,384]{2,0,1:T(8,128)} %fusion.13), kind=kOutput, calls=%fused_computation.6 | convolution fusion | flops 9082699776 | bytes 35000832 | tf_op jit(solution)/shard_map/cjh,jhd->cjd/dot_general | solution.py:94
  252.5 0.0 reduce-scatter.4.cloned.1.call-update
  252.6 0.0 reduce-scatter.8.cloned.1.call-start
  252.6 0.6 copy-done.4
  253.2 0.1 compare_reduce_fusion.1
  253.3 1.4 constant_dynamic-slice_fusion
  254.7 3.2 fusion.56
  257.9 4.3 convolution_convert_fusion.1
  262.3 0.0 reduce-scatter.6.cloned.1.call-start
  262.4 0.6 reduce-window.14
  263.0 0.2 slice_reduce_fusion.1
  263.2 0.2 reduce-window.15
  263.4 0.1 fusion.37
  263.5 0.2 copy.54
  263.6 0.2 reshape.166
  263.8 0.1 add_bitcast_fusion
  263.9 0.1 multiply_reduce_fusion.1
  264.0 0.1 and_reduce_fusion.1
  264.1 0.1 copy.43
  264.3 0.2 reshape.152
  264.4 4.3 scatter_custom_fusion.3
  268.7 0.1 reshape.129
  268.9 0.2 reshape.154
  269.0 4.3 scatter_custom_fusion.1
  273.3 0.1 reshape.121
  273.4 0.1 copy.44
  273.6 0.1 reshape.113
  273.7 117.1 %reduce-scatter.4.cloned.1.call-done = bf16[288,2,2560]{2,0,1:T(8,128)(2,1)} async-done(((bf16[1152,2,2560]{2,0,1:T(8,128)(2,1)}), bf16[288,2,2560]{2,0,1:T(8,128)(2,1)}) %reduce-scatter.4.cloned.1.call-update) | async-done | bytes 2949136 | tf_op jit(solution)/shard_map/reduce_scatter | solution.py:93
  390.9 2.3 convert_multiply_fusion.2
  393.2 7.1 %copy.55 = f32[288,2,2560]{2,1,0:T(2,128)} copy(f32[288,2,2560]{2,0,1:T(8,128)S(1)} %convert_multiply_fusion.2) | data formatting | bytes 11796480 | tf_op jit(solution)/shard_map/mul | solution.py:111
  400.3 8.3 %reshape.148 = f32[576,2560]{1,0:T(8,128)} reshape(f32[288,2,2560]{2,1,0:T(2,128)} %copy.55) | data formatting | bytes 11796480 | tf_op jit(solution)/shard_map/reshape | solution.py:111
  408.5 20.4 %scatter_custom_fusion = f32[512,2560]{1,0:T(8,128)} fusion(s32[576]{0:T(1024)S(1)} %fusion.43, f32[576,2560]{1,0:T(8,128)} %reshape.148, f32[]{:T(128)} %constant.17.clone.1), kind=kCustom, calls=%fused_computation.26 | custom fusion | flops 1474560 | bytes 5243392 | tf_op jit(solution)/shard_map/scatter-add | solution.py:115
  429.0 4.3 convert_element_type.68
  433.3 0.0 reduce-scatter.8.cloned.1.call-done
  433.3 37.7 %reduce-scatter.6.cloned.1.call-done = bf16[64,2560]{1,0:T(8,128)(2,1)} async-done(((bf16[512,2560]{1,0:T(8,128)(2,1)}), bf16[64,2560]{1,0:T(8,128)(2,1)}) %reduce-scatter.6.cloned.1.call-update) | async-done | bytes 327696 | tf_op jit(solution)/shard_map/reduce_scatter | solution.py:117
  471.0 1.9 add_convert_fusion
  (47 shorter events, 0.4 us)
Async XLA Ops:
  6.5 251.4 %copy-start = (bf16[384,2560]{1,0:T(8,128)(2,1)S(1)}, bf16[384,2560]{1,0:T(8,128)(2,1)}, u32[]{:S(2)}) copy-start(bf16[384,2560]{1,0:T(8,128)(2,1)} %param.21) | copy-start | bytes 5898244
  6.5 113.5 %all-gather.2.cloned.1.call-start = ((), (), s32[]{:S(2)}) async-start(), calls=%async_computation.3 | async-start | bytes 13107200 | tf_op jit(solution)/shard_map/all_gather | solution.py:74
  6.5 2.7 copy-start.1
  9.2 3.0 copy-start.2
  9.2 16.5 %copy-start.6 = (s32[3]{0:T(128)S(1)}, s32[3]{0:T(128)}, u32[]{:S(2)}) copy-start(s32[3]{0:T(128)} %constant.77) | copy-start | bytes 40
  9.2 16.6 %copy-start.5 = (s32[3]{0:T(128)S(1)}, s32[3]{0:T(128)}, u32[]{:S(2)}) copy-start(s32[3]{0:T(128)} %constant.80) | copy-start | bytes 40
  12.2 378.7 %reduce-scatter.4.cloned.1.call-start = ((), (), s32[]{:S(2)}) async-start(), calls=%async_computation.4 | async-start | bytes 14745600 | tf_op jit(solution)/shard_map/reduce_scatter | solution.py:93
  252.5 0.7 copy-start.4
  252.6 180.7 %reduce-scatter.8.cloned.1.call-start = ((), (), s32[]{:S(2)}) async-start(), calls=%async_computation.6 | async-start | bytes 1638400 | tf_op jit(solution)/shard_map/reduce_scatter | solution.py:105
  257.9 5.5 %copy-start.3 = (bf16[512,6]{0,1:T(8,128)(2,1)S(1)}, bf16[512,6]{0,1:T(8,128)(2,1)}, u32[]{:S(2)}) copy-start(bf16[512,6]{0,1:T(8,128)(2,1)} %param.13) | copy-start | bytes 18436
  257.9 6.0 %copy-start.7 = (s32[2]{0:T(128)S(1)}, s32[2]{0:T(128)}, u32[]{:S(2)}) copy-start(s32[2]{0:T(128)} %constant.44) | copy-start | bytes 28
  257.9 6.1 %copy-start.8 = (s32[2]{0:T(128)S(1)}, s32[2]{0:T(128)}, u32[]{:S(2)}) copy-start(s32[2]{0:T(128)} %constant.74) | copy-start | bytes 28
  262.3 208.7 %reduce-scatter.6.cloned.1.call-start = ((), (), s32[]{:S(2)}) async-start(), calls=%async_computation.5 | async-start | bytes 2949120 | tf_op jit(solution)/shard_map/reduce_scatter | solution.py:117
Sparse Core Ops, SparseCore 0:
  12.3 107.7 all-gather.1
  252.7 138.1 reduce-scatter.3
  393.8 29.3 reduce-scatter.7
  433.4 37.5 reduce-scatter.5
where the time goes:
time: 484 us; the launch traced here: 480 us
  waiting for transfers between devices  231 us (48%)
  local copies, waits for them, and re-layouts  144 us (30%)
  matrix products  41.6 us (9%)
  other arithmetic  39.2 us (8%)
  between operations  13.9 us (3%)
  blocking collectives  9.62 us (2%)
    reduce_scatter x1, waiting for transfers between devices, on_device(): lax.psum_scatter(jnp.einsum('cjh,jhd->cjd', hidden, expert_down, preferre...  117 us
    gather x4, local copies, waits for them, and re-layouts, pick_rows(): jnp.take(normed_block, jnp.minimum(slot_token, row_count - 1), axis=0)  98.9 us
    all_gather x1, waiting for transfers between devices, on_device(): lax.all_gather(normed, 'seq', axis=0, tiled=True)  76 us
    reduce_scatter x1, waiting for transfers between devices, on_device(): lax.psum_scatter(routed_local.astype(jnp.bfloat16), 'tp', scatter_dimensi...  37.7 us
    unnamed x28, local copies, waits for them, and re-layouts  26.4 us
    dot_general x1, matrix products, on_device(): jnp.einsum('cjh,jhd->cjd', hidden, expert_down, preferred_element_type=jn...  21.3 us
    scatter-add x1, other arithmetic, on_device(): routed_local = jnp.zeros((tok_seq, width), jnp.float32).at[own_token.resh...  20.4 us
    dot_general x1, matrix products, on_device(): jnp.einsum('cjd,jhd->cjh', piece, expert_gate, preferred_element_type=jnp...  12.8 us
  transfers between devices with their start and end apart: 4, of which 3 were waited for; matrix products, arithmetic and copies ran while one was open for 18% of the time, Pallas kernels for 0%

commit v1 on v0

v1 whole, which is shorter than its diff:
```python
from functools import partial

import jax
import jax.numpy as jnp
from jax import lax
from jax.experimental import pallas as pl
from jax.experimental.pallas import tpu as pltpu
from jax.sharding import PartitionSpec as P

MESH = pl.DeviceIdType.MESH
LANES = 128


def rms_rows(tokens, norm_gain):
    values = tokens.astype(jnp.float32)
    scale = lax.rsqrt(jnp.mean(values * values, axis=-1, keepdims=True) + 1e-05)
    return (values * scale * norm_gain).astype(jnp.bfloat16)


def dot_nt(a, b):
    return lax.dot_general(a, b, (((1,), (1,)), ((), ())), preferred_element_type=jnp.float32)


def silu(v):
    return v / (1.0 + jnp.exp(-v))


def layer_kernel(
    chunks,
    n_z,
    columns,
    width,
    rows_z,
    own_hbm,
    gate_hbm,
    up_hbm,
    down_hbm,
    sgate_hbm,
    sup_hbm,
    sdown_hbm,
    out_ref,
    x_buf,
    part,
    from_sib,
    ring_in,
    z_in,
    gate_w,
    up_w,
    down_w,
    sgate_w,
    sup_w,
    sdown_w,
    hid,
    shid,
    w_sem,
    own_sem,
    send_own,
    send_fwd,
    send_part,
    send_ring,
    send_z,
    recv_x,
    recv_part,
    recv_ring,
    recv_z,
):
    seq = lax.axis_index("seq")
    tp = lax.axis_index("tp")
    core = tp % 2
    zed = tp // 2
    other = 1 - core
    sx = seq % 2
    sy = seq // 2
    nbr_x = sy * 2 + (1 - sx)
    nbr_y = (1 - sy) * 2 + sx
    blk_a = nbr_y * other + nbr_x * core
    blk_b = nbr_x * other + nbr_y * core
    blk_d = 3 - seq
    sib = (seq, zed * 2 + other)
    dev_a = (blk_a, tp)
    dev_b = (blk_b, tp)
    rows = n_z * rows_z
    inner = gate_w.shape[1]

    def remote(src, dst, ssem, rsem, dev):
        return pltpu.make_async_remote_copy(
            src_ref=src, dst_ref=dst, send_sem=ssem, recv_sem=rsem, device_id=dev, device_id_type=MESH
        )

    def own_copy(k, slot, dev):
        return remote(
            own_hbm.at[k], x_buf.at[seq, k, core], send_own.at[k, slot], recv_x.at[k, seq, core], dev
        )

    def x_copy(k, blk, half, slot, dev):
        return remote(
            x_buf.at[blk, k, half],
            x_buf.at[blk, k, half],
            send_fwd.at[k, slot],
            recv_x.at[k, blk, half],
            dev,
        )

    def part_copy(k, blk):
        return remote(
            part.at[blk, k, other],
            from_sib.at[blk, k],
            send_part.at[k, blk],
            recv_part.at[k, blk],
            sib,
        )

    def ring_copy(k, blk, slot, dev):
        return remote(
            part.at[blk, k, core],
            ring_in.at[k, slot],
            send_ring.at[k, slot],
            recv_ring.at[k, slot],
            dev,
        )

    def z_copy(k, src_z, dst_z):
        return remote(
            part.at[seq, k, core, pl.ds(dst_z * rows_z, rows_z)],
            z_in.at[k, src_z],
            send_z.at[k, dst_z],
            recv_z.at[k, src_z],
            (seq, dst_z * 2 + core),
        )

    weight_copies = [
        pltpu.make_async_copy(src, dst, w_sem.at[i])
        for i, (src, dst) in enumerate(
            (
                (gate_hbm, gate_w),
                (up_hbm, up_w),
                (down_hbm, down_w),
                (sgate_hbm, sgate_w),
                (sup_hbm, sup_w),
                (sdown_hbm, sdown_w),
            )
        )
    ]

    def local_own(k):
        return pltpu.make_async_copy(own_hbm.at[k], x_buf.at[seq, k, core], own_sem.at[k])

    barrier = pltpu.get_barrier_semaphore()
    for dev in (sib, dev_a, dev_b):
        pl.semaphore_signal(barrier, inc=1, device_id=dev, device_id_type=MESH)
    for step in range(1, n_z):
        target = (zed + step) % n_z
        pl.semaphore_signal(
            barrier, inc=1, device_id=(seq, target * 2 + core), device_id_type=MESH
        )
    for k in range(chunks):
        local_own(k).start()
    pl.semaphore_wait(barrier, 3 + n_z - 1)

    for k in range(chunks):
        if k < 2:
            own_copy(k, 1, dev_a).start()
            own_copy(k, 2, dev_b).start()
        own_copy(k, 0, sib).start()
    for copy in weight_copies:
        copy.start()
    for k in range(chunks):
        local_own(k).wait()
    for copy in weight_copies:
        copy.wait()

    def unit(k, blk):
        x_all = x_buf[blk, k].reshape(2 * rows, x_buf.shape[-1])
        x = x_all[:, :width]
        listed = x_all[:, width:].astype(jnp.float32)
        lane = lax.broadcasted_iota(jnp.int32, listed.shape, 1)
        for i in range(columns):
            mine = jnp.where(lane == tp * columns + i, listed, 0.0)
            weight = jnp.sum(mine, axis=1, keepdims=True)
            g = dot_nt(x, gate_w[i])
            u = dot_nt(x, up_w[i])
            hid[:, i * inner : (i + 1) * inner] = (silu(g) * u * weight).astype(jnp.bfloat16)
        tile = 512

        @pl.loop(0, width // tile)
        def _(n):
            cols = pl.ds(pl.multiple_of(n * tile, tile), tile)
            p = jnp.dot(hid[...], down_w[:, cols], preferred_element_type=jnp.float32)
            part[blk, k, :, :, cols] = p.astype(jnp.bfloat16).reshape(2, rows, tile)

        part_copy(k, blk).start()

    def shared(k):
        mine = pl.ds(pl.multiple_of(zed * rows_z, rows_z), rows_z)
        x = jnp.concatenate([x_buf[b, k, core, mine, :width] for b in range(4)], axis=0)
        shid[...] = (silu(dot_nt(x, sgate_w[...])) * dot_nt(x, sup_w[...])).astype(jnp.bfloat16)
        tile = 512

        @pl.loop(0, width // tile)
        def _(n):
            cols = pl.ds(pl.multiple_of(n * tile, tile), tile)
            p = jnp.dot(shid[...], sdown_w[:, cols], preferred_element_type=jnp.float32)
            for b in range(4):
                old = part[b, k, core, mine, cols].astype(jnp.float32)
                new = old + p[b * rows_z : (b + 1) * rows_z]
                part[b, k, core, mine, cols] = new.astype(jnp.bfloat16)

    def add_pair(k, blk):
        part_copy(k, blk).wait_recv()
        total = part[blk, k, core].astype(jnp.float32) + from_sib[blk, k].astype(jnp.float32)
        part[blk, k, core] = total.astype(jnp.bfloat16)

    def ring_one(k):
        add_pair(k, blk_d)
        ring_copy(k, blk_d, 0, dev_a).start()
        add_pair(k, blk_a)
        ring_copy(k, blk_a, 1, dev_a).start()
        add_pair(k, blk_b)
        add_pair(k, seq)

    def ring_two(k):
        ring_copy(k, blk_d, 0, dev_a).wait_recv()
        total = part[blk_b, k, core].astype(jnp.float32) + ring_in[k, 0].astype(jnp.float32)
        part[blk_b, k, core] = total.astype(jnp.bfloat16)
        ring_copy(k, blk_b, 2, dev_b).start()

    def ring_three(k):
        ring_copy(k, blk_a, 1, dev_a).wait_recv()
        ring_copy(k, blk_b, 2, dev_b).wait_recv()
        total = (
            part[seq, k, core].astype(jnp.float32)
            + ring_in[k, 1].astype(jnp.float32)
            + ring_in[k, 2].astype(jnp.float32)
        )
        part[seq, k, core] = total.astype(jnp.bfloat16)
        for step in range(1, n_z):
            z_copy(k, zed, (zed + step) % n_z).start()

    def finish(k):
        total = part[
            seq, k, core, pl.ds(pl.multiple_of(zed * rows_z, rows_z), rows_z)
        ].astype(jnp.float32)
        for step in range(1, n_z):
            source = (zed + step) % n_z
            z_copy(k, source, source).wait_recv()
            total = total + z_in[k, source].astype(jnp.float32)
        out_ref[k] = total.astype(jnp.bfloat16)

    @pl.loop(0, chunks)
    def _(k):
        own_copy_in = x_copy(k, seq, other, 0, sib)
        own_copy_in.wait_recv()
        unit(k, seq)
        x_copy(k, blk_b, core, 0, sib).wait_recv()
        x_copy(k, blk_b, core, 3, dev_a).start()
        x_copy(k, blk_b, core, 1, sib).start()
        x_copy(k, blk_a, core, 0, sib).wait_recv()
        x_copy(k, blk_a, core, 0, sib).start()

        @pl.when(k + 2 < chunks)
        def _():
            own_copy(k + 2, 1, dev_a).start()
            own_copy(k + 2, 2, dev_b).start()

        @pl.when(k > 0)
        def _():
            ring_two(k - 1)

        x_copy(k, blk_b, other, 0, sib).wait_recv()
        unit(k, blk_b)
        x_copy(k, blk_a, other, 0, sib).wait_recv()
        unit(k, blk_a)
        x_copy(k, blk_d, core, 0, sib).wait_recv()
        x_copy(k, blk_d, core, 2, sib).start()

        @pl.when(k > 0)
        def _():
            ring_three(k - 1)

        x_copy(k, blk_d, other, 0, sib).wait_recv()
        unit(k, blk_d)
        shared(k)
        ring_one(k)

    ring_two(chunks - 1)
    ring_three(chunks - 1)

    @pl.loop(0, chunks)
    def _(k):
        finish(k)
        own_copy(k, 0, sib).wait_send()
        own_copy(k, 1, dev_a).wait_send()
        own_copy(k, 2, dev_b).wait_send()
        x_copy(k, blk_a, core, 0, sib).wait_send()
        x_copy(k, blk_b, core, 1, sib).wait_send()
        x_copy(k, blk_d, core, 2, sib).wait_send()
        x_copy(k, blk_b, core, 3, dev_a).wait_send()
        for b in range(4):
            part_copy(k, b).wait_send()
        ring_copy(k, blk_d, 0, dev_a).wait_send()
        ring_copy(k, blk_a, 1, dev_a).wait_send()
        ring_copy(k, blk_b, 2, dev_b).wait_send()
        for step in range(1, n_z):
            z_copy(k, zed, (zed + step) % n_z).wait_send()


def on_device(
    tokens,
    expert_ids,
    gate_weights,
    live,
    norm_gain,
    expert_gate,
    expert_up,
    expert_down,
    shared_gate,
    shared_up,
    shared_down,
):
    tok_seq, width = tokens.shape
    columns, inner = expert_gate.shape[:2]
    s_inner = shared_gate.shape[0]
    n_seq = lax.axis_size("seq")
    n_tp = lax.axis_size("tp")
    assert n_seq == 4
    tok_dev = tok_seq // n_tp
    n_z = n_tp // 2
    chunks = max(1, min(2, tok_dev // 16))
    rows_z = tok_dev // chunks
    rows = n_z * rows_z
    experts = columns * n_tp
    pad = -(-experts // LANES) * LANES
    core = lax.axis_index("tp") % 2

    def half(a):
        split = a.reshape((n_z, 2, chunks, rows_z) + a.shape[1:])
        picked = lax.dynamic_index_in_dim(split, core, 1, keepdims=False)
        return jnp.swapaxes(picked, 0, 1).reshape((chunks * rows,) + a.shape[1:])

    normed = rms_rows(half(tokens), norm_gain)
    ids = half(expert_ids)
    weights = half(gate_weights).astype(jnp.float32) * half(live).astype(jnp.float32)[:, None]
    matches = ids[:, :, None] == jnp.arange(pad, dtype=jnp.int32)[None, None, :]
    listed = jnp.sum(jnp.where(matches, weights[:, :, None], 0.0), axis=1).astype(jnp.bfloat16)
    own = jnp.concatenate([normed, listed], axis=1).reshape(chunks, rows, width + pad)

    bf16 = jnp.bfloat16
    dma = pltpu.SemaphoreType.DMA
    out = pl.pallas_call(
        partial(layer_kernel, chunks, n_z, columns, width, rows_z),
        out_shape=jax.ShapeDtypeStruct((chunks, rows_z, width), bf16),
        in_specs=[pl.BlockSpec(memory_space=pl.ANY)] * 7,
        out_specs=pl.BlockSpec(memory_space=pltpu.VMEM),
        scratch_shapes=[
            pltpu.VMEM((4, chunks, 2, rows, width + pad), bf16),
            pltpu.VMEM((4, chunks, 2, rows, width), bf16),
            pltpu.VMEM((4, chunks, rows, width), bf16),
            pltpu.VMEM((chunks, 3, rows, width), bf16),
            pltpu.VMEM((chunks, n_z, rows_z, width), bf16),
            pltpu.VMEM((columns, inner, width), bf16),
            pltpu.VMEM((columns, inner, width), bf16),
            pltpu.VMEM((columns * inner, width), bf16),
            pltpu.VMEM((s_inner, width), bf16),
            pltpu.VMEM((s_inner, width), bf16),
            pltpu.VMEM((s_inner, width), bf16),
            pltpu.VMEM((2 * rows, columns * inner), bf16),
            pltpu.VMEM((4 * rows_z, s_inner), bf16),
            dma((6,)),
            dma((chunks,)),
            dma((chunks, 3)),
            dma((chunks, 4)),
            dma((chunks, 4)),
            dma((chunks, 3)),
            dma((chunks, n_z)),
            dma((chunks, 4, 2)),
            dma((chunks, 4)),
            dma((chunks, 3)),
            dma((chunks, n_z)),
        ],
        compiler_params=pltpu.CompilerParams(
            collective_id=0, has_side_effects=True, vmem_limit_bytes=62 * 1024 * 1024
        ),
    )(
        own,
        expert_gate,
        expert_up,
        expert_down.reshape(columns * inner, width),
        shared_gate,
        shared_up,
        shared_down,
    )
    return out.reshape(tok_dev, width)


def solution(mesh):
    placed = (
        P("seq", None),
        P("seq", None),
        P("seq", None),
        P("seq"),
        P(),
        P("tp", "seq", None),
        P("tp", "seq", None),
        P("tp", "seq", None),
        P("seq", None),
        P("seq", None),
        P("seq", None),
    )
    return jax.shard_map(
        on_device, mesh=mesh, in_specs=placed, out_specs=P(("seq", "tp"), None), check_vma=False
    )
```

time: 484 us -> 141 us (0.29)
  waiting for transfers between devices: 231 us -> 0 us
  local copies, waits for them, and re-layouts: 144 us -> 2.74 us
  Pallas kernels: 0 us -> 131 us
  matrix products: 41.6 us -> 0 us
  other arithmetic: 39.2 us -> 6.56 us
  between operations: 13.9 us -> 0.08 us
  blocking collectives: 9.62 us -> 0 us
    reduce_scatter x3 -> x0, waiting for transfers between devices: 155 us -> none  [the longest x1 117 us: on_device(): lax.psum_scatter(jnp.einsum('cjh,jhd->cjd', hidden, expert_down, preferre...]
    pallas_call x0 -> x1, Pallas kernels: none -> 131 us  [on_device(): pl.pallas_call(partial(layer_kernel, chunks, n_z, columns, width, rows_z)...]
    gather x4 -> x0, local copies, waits for them, and re-layouts: 98.9 us -> none  [pick_rows(): jnp.take(normed_block, jnp.minimum(slot_token, row_count - 1), axis=0)]
    all_gather x1 -> x0, waiting for transfers between devices: 76 us -> none  [on_device(): lax.all_gather(normed, 'seq', axis=0, tiled=True)]
    dot_general x4 -> x0, matrix products: 41.6 us -> none  [the longest x1 21.3 us: on_device(): jnp.einsum('cjh,jhd->cjd', hidden, expert_down, preferred_element_type=jn...]
    unnamed x28 -> x11, local copies, waits for them, and re-layouts: 26.4 us -> 2.09 us
    scatter-add x1 -> x0, other arithmetic: 20.4 us -> none  [on_device(): routed_local = jnp.zeros((tok_seq, width), jnp.float32).at[own_token.resh...]
    all_gather x1 -> x0, blocking collectives: 9.62 us -> none  [on_device(): lax.all_gather(expert_ids.astype(jnp.bfloat16), 'seq', axis=0, tiled=True)]
  transfers between devices with their start and end apart: 4 -> 0, of which waited for: 3 -> 0; matrix products, arithmetic and copies ran while one was open for 18% -> 0% of each run, Pallas kernels for 0% -> 0%
where the time goes in v1:
time: 141 us; the launch traced here: 140 us
  Pallas kernels  131 us (93%)
  other arithmetic  6.56 us (5%)
  local copies, waits for them, and re-layouts  2.74 us (2%)
    pallas_call x1, Pallas kernels, on_device(): pl.pallas_call(partial(layer_kernel, chunks, n_z, columns, width, rows_z)...  131 us

profile of v1, /device:TPU:0, one launch (start us, length us, event | category | flops | bytes accessed | tf_op | source)
XLA Modules:
  0.0 140.3 jit_solution(10342641721311584046)
XLA Ops:
  0.0 0.0 copy-start
  0.0 0.0 copy-start.2
  0.0 1.8 %copy_convert_fusion = f32[4,1,2,32,2560]{4,3,0,2,1:T(8,128)S(1)} fusion(bf16[4,2,2,32,2560]{4,3,2,1,0:T(8,128)(2,1)} %bitcast.37, s32[]{:T(128)S(6)} %select_n.22), kind=kLoop, calls=%fused_computation.3 | loop fusion | flops 655360 | bytes 3932164 | tf_op jit(solution)/shard_map/convert_element_type | solution.py:15
  1.8 0.4 copy-done
  2.1 0.0 copy-start.1
  2.1 0.0 copy-start.3
  2.1 0.0 copy-start.4
  2.1 0.3 multiply_reduce_fusion
  2.5 0.1 rsqrt.12
  2.6 0.0 copy-done.2
  2.6 1.4 multiply_convert_fusion
  3.9 0.0 copy-done.1
  4.0 0.1 reshape.94
  4.1 0.1 eq.17
  4.2 0.0 copy-done.3
  4.2 0.1 reshape.95
  4.3 0.1 reshape.100
  4.4 0.0 copy-done.4
  4.4 0.1 reshape.96
  4.5 0.1 convert_element_type.74
  4.6 0.6 select_reduce_fusion
  5.2 2.5 %pad_maximum_fusion.own_hbm = bf16[2,128,2688]{2,1,0:T(8,128)(2,1)} fusion(bf16[2,128,128]{2,1,0:T(8,128)(2,1)S(1)} %bitcast.40, bf16[2,128,2560]{2,1,0:T(8,128)(2,1)} %multiply_convert_fusion), kind=kLoop, calls=%fused_computation.2 | loop fusion | flops 2752512 | bytes 2752512 | tf_op jit(solution)/shard_map/concatenate | solution.py:345
  7.7 130.9 %shard_map.109 = bf16[2,32,2560]{2,1,0:T(8,128)(2,1)} custom-call(bf16[2,128,2688]{2,1,0:T(8,128)(2,1)} %pad_maximum_fusion.own_hbm, bf16[2,384,2560]{2,1,0:T(8,128)(2,1)} %gate_hbm.1, bf16[2,384,2560]{2,1,0:T(8,128)(2,1)} %up_hbm.1, bf16[768,2560]{1,0:T(8,128)(2,1)} %bitcast.36, bf16[384,2560]{1,0:T(8,128)(2,1)} %sgate_hbm.1, bf16[384,2560]{1,0:T(8,128)(2,1)} %sup_hbm.1, ...), custom_call_target="tpu_custom_call" | custom-call | tf_op jit(solution)/shard_map/pallas_call | solution.py:349
  138.6 1.7 %copy.39 = bf16[64,2560]{1,0:T(8,128)(2,1)} copy(bf16[64,2560]{1,0:T(8,128)(2,1)} %bitcast.39) | data formatting | bytes 655360
  (8 shorter events, 0.1 us)
Async XLA Ops:
  0.0 2.1 %copy-start = (bf16[512,2560]{1,0:T(8,128)(2,1)S(1)}, bf16[512,2560]{1,0:T(8,128)(2,1)}, u32[]{:S(2)}) copy-start(bf16[512,2560]{1,0:T(8,128)(2,1)} %param.11) | copy-start | bytes 7864324
  0.0 2.6 %copy-start.2 = (f32[2560]{0:T(1024)S(1)}, f32[2560]{0:T(1024)}, u32[]{:S(2)}) copy-start(f32[2560]{0:T(1024)} %param.15) | copy-start | bytes 30724
  2.1 1.8 %copy-start.1 = (s32[512,6]{0,1:T(8,128)S(1)}, s32[512,6]{0,1:T(8,128)}, u32[]{:S(2)}) copy-start(s32[512,6]{0,1:T(8,128)} %param.12) | copy-start | bytes 36868
  2.1 2.0 %copy-start.3 = (bf16[512,6]{0,1:T(8,128)(2,1)S(1)}, bf16[512,6]{0,1:T(8,128)(2,1)}, u32[]{:S(2)}) copy-start(bf16[512,6]{0,1:T(8,128)(2,1)} %param.13) | copy-start | bytes 18436
  2.1 2.3 %copy-start.4 = (s32[512]{0:T(512)S(1)}, s32[512]{0:T(512)}, u32[]{:S(2)}) copy-start(s32[512]{0:T(512)} %param.14) | copy-start | bytes 6148

commit v2 on v1

--- a/solution.py
+++ b/solution.py
@@ -11,12 +11,6 @@
 LANES = 128
 
 
-def rms_rows(tokens, norm_gain):
-    values = tokens.astype(jnp.float32)
-    scale = lax.rsqrt(jnp.mean(values * values, axis=-1, keepdims=True) + 1e-05)
-    return (values * scale * norm_gain).astype(jnp.bfloat16)
-
-
 def dot_nt(a, b):
     return lax.dot_general(a, b, (((1,), (1,)), ((), ())), preferred_element_type=jnp.float32)
 
@@ -31,7 +25,11 @@
     columns,
     width,
     rows_z,
-    own_hbm,
+    share,
+    ahead,
+    tok_hbm,
+    gain_ref,
+    listed_ref,
     gate_hbm,
     up_hbm,
     down_hbm,
@@ -52,6 +50,7 @@
     sdown_w,
     hid,
     shid,
+    tok_v,
     w_sem,
     own_sem,
     send_own,
@@ -80,6 +79,11 @@
     dev_a = (blk_a, tp)
     dev_b = (blk_b, tp)
     rows = n_z * rows_z
+    parity = zed % 2
+    dev_z = (seq, (zed + 1 - 2 * parity) * 2 + core)
+    fetched = pl.ds(pl.multiple_of(parity * share, 16), rows - share)
+    passed = pl.ds(pl.multiple_of(parity * (rows - share), 16), share)
+    given = pl.ds(pl.multiple_of((1 - parity) * (rows - share), 16), share)
     inner = gate_w.shape[1]
 
     def remote(src, dst, ssem, rsem, dev):
@@ -88,18 +92,45 @@
         )
 
     def own_copy(k, slot, dev):
-        return remote(
-            own_hbm.at[k], x_buf.at[seq, k, core], send_own.at[k, slot], recv_x.at[k, seq, core], dev
-        )
-
-    def x_copy(k, blk, half, slot, dev):
-        return remote(
-            x_buf.at[blk, k, half],
-            x_buf.at[blk, k, half],
-            send_fwd.at[k, slot],
-            recv_x.at[k, blk, half],
-            dev,
-        )
+        return x_copy(k, seq, core, fetched, send_own.at[k, slot], 0, dev)
+
+    def own_sib(k, half):
+        return x_copy(k, seq, half, pl.ds(0, rows), send_own.at[k, 0], 2, sib)
+
+    def x_copy(k, blk, half, span, ssem, kind, dev):
+        ref = x_buf.at[blk, k, half, span]
+        return remote(ref, ref, ssem, recv_x.at[k, blk, kind], dev)
+
+    def net(k, blk):
+        return x_copy(k, blk, core, fetched, send_fwd.at[k, 0], 0, dev_a)
+
+    def relay(k):
+        return x_copy(k, blk_b, core, fetched, send_fwd.at[k, 0], 0, dev_a)
+
+    def over_z(k, blk, slot):
+        return x_copy(k, blk, core, passed, send_fwd.at[k, slot], 1, dev_z)
+
+    def from_z(k, blk):
+        return x_copy(k, blk, core, given, send_fwd.at[k, 0], 1, dev_z)
+
+    def sib_net(k, blk, half, slot):
+        return x_copy(k, blk, half, fetched, send_fwd.at[k, slot], 2, sib)
+
+    def sib_z(k, blk, half, slot):
+        return x_copy(k, blk, half, given, send_fwd.at[k, slot], 3, sib)
+
+    def got_net(k, blk, slot):
+        net(k, blk).wait_recv()
+        over_z(k, blk, slot).start()
+        sib_net(k, blk, core, slot + 3).start()
+
+    def got_z(k, blk, slot):
+        from_z(k, blk).wait_recv()
+        sib_z(k, blk, core, slot + 6).start()
+
+    def got_sib(k, blk):
+        sib_net(k, blk, other, 0).wait_recv()
+        sib_z(k, blk, other, 0).wait_recv()
 
     def part_copy(k, blk):
         return remote(
@@ -142,8 +173,14 @@
         )
     ]
 
-    def local_own(k):
-        return pltpu.make_async_copy(own_hbm.at[k], x_buf.at[seq, k, core], own_sem.at[k])
+    def load_own(k):
+        return pltpu.make_async_copy(tok_hbm.at[:, core, k], tok_v.at[k], own_sem.at[k])
+
+    def norm_own(k):
+        values = tok_v[k].reshape(rows, width).astype(jnp.float32)
+        scale = lax.rsqrt(jnp.mean(values * values, axis=-1, keepdims=True) + 1e-05)
+        x_buf[seq, k, core, :, :width] = (values * scale * gain_ref[...]).astype(jnp.bfloat16)
+        x_buf[seq, k, core, :, width:] = listed_ref[k]
 
     barrier = pltpu.get_barrier_semaphore()
     for dev in (sib, dev_a, dev_b):
@@ -154,18 +191,18 @@
             barrier, inc=1, device_id=(seq, target * 2 + core), device_id_type=MESH
         )
     for k in range(chunks):
-        local_own(k).start()
-    pl.semaphore_wait(barrier, 3 + n_z - 1)
-
+        load_own(k).start()
     for k in range(chunks):
-        if k < 2:
+        load_own(k).wait()
+        norm_own(k)
+        if k == 0:
+            pl.semaphore_wait(barrier, 3 + n_z - 1)
+        if k < ahead:
             own_copy(k, 1, dev_a).start()
             own_copy(k, 2, dev_b).start()
-        own_copy(k, 0, sib).start()
+        own_sib(k, core).start()
     for copy in weight_copies:
         copy.start()
-    for k in range(chunks):
-        local_own(k).wait()
     for copy in weight_copies:
         copy.wait()
 
@@ -246,38 +283,50 @@
             total = total + z_in[k, source].astype(jnp.float32)
         out_ref[k] = total.astype(jnp.bfloat16)
 
+    def service(k):
+        net(k, blk_b).wait_recv()
+        relay(k).start()
+        over_z(k, blk_b, 2).start()
+        sib_net(k, blk_b, core, 5).start()
+        got_net(k, blk_a, 1)
+
+        @pl.when(k + ahead < chunks)
+        def _():
+            own_copy(k + ahead, 1, dev_a).start()
+            own_copy(k + ahead, 2, dev_b).start()
+
     @pl.loop(0, chunks)
     def _(k):
-        own_copy_in = x_copy(k, seq, other, 0, sib)
-        own_copy_in.wait_recv()
+        own_sib(k, other).wait_recv()
         unit(k, seq)
-        x_copy(k, blk_b, core, 0, sib).wait_recv()
-        x_copy(k, blk_b, core, 3, dev_a).start()
-        x_copy(k, blk_b, core, 1, sib).start()
-        x_copy(k, blk_a, core, 0, sib).wait_recv()
-        x_copy(k, blk_a, core, 0, sib).start()
-
-        @pl.when(k + 2 < chunks)
+
+        @pl.when(k == 0)
         def _():
-            own_copy(k + 2, 1, dev_a).start()
-            own_copy(k + 2, 2, dev_b).start()
+            service(k)
 
         @pl.when(k > 0)
         def _():
             ring_two(k - 1)
 
-        x_copy(k, blk_b, other, 0, sib).wait_recv()
+        got_z(k, blk_b, 2)
+        got_z(k, blk_a, 1)
+        got_sib(k, blk_b)
         unit(k, blk_b)
-        x_copy(k, blk_a, other, 0, sib).wait_recv()
+        got_net(k, blk_d, 3)
+        got_sib(k, blk_a)
         unit(k, blk_a)
-        x_copy(k, blk_d, core, 0, sib).wait_recv()
-        x_copy(k, blk_d, core, 2, sib).start()
 
         @pl.when(k > 0)
         def _():
             ring_three(k - 1)
 
-        x_copy(k, blk_d, other, 0, sib).wait_recv()
+        got_z(k, blk_d, 3)
+        got_sib(k, blk_d)
+
+        @pl.when(k + 1 < chunks)
+        def _():
+            service(k + 1)
+
         unit(k, blk_d)
         shared(k)
         ring_one(k)
@@ -288,13 +337,14 @@
     @pl.loop(0, chunks)
     def _(k):
         finish(k)
-        own_copy(k, 0, sib).wait_send()
+        own_sib(k, core).wait_send()
         own_copy(k, 1, dev_a).wait_send()
         own_copy(k, 2, dev_b).wait_send()
-        x_copy(k, blk_a, core, 0, sib).wait_send()
-        x_copy(k, blk_b, core, 1, sib).wait_send()
-        x_copy(k, blk_d, core, 2, sib).wait_send()
-        x_copy(k, blk_b, core, 3, dev_a).wait_send()
+        relay(k).wait_send()
+        for slot, blk in ((1, blk_a), (2, blk_b), (3, blk_d)):
+            over_z(k, blk, slot).wait_send()
+            sib_net(k, blk, core, slot + 3).wait_send()
+            sib_z(k, blk, core, slot + 6).wait_send()
         for b in range(4):
             part_copy(k, b).wait_send()
         ring_copy(k, blk_d, 0, dev_a).wait_send()
@@ -337,19 +387,24 @@
         picked = lax.dynamic_index_in_dim(split, core, 1, keepdims=False)
         return jnp.swapaxes(picked, 0, 1).reshape((chunks * rows,) + a.shape[1:])
 
-    normed = rms_rows(half(tokens), norm_gain)
     ids = half(expert_ids)
     weights = half(gate_weights).astype(jnp.float32) * half(live).astype(jnp.float32)[:, None]
     matches = ids[:, :, None] == jnp.arange(pad, dtype=jnp.int32)[None, None, :]
     listed = jnp.sum(jnp.where(matches, weights[:, :, None], 0.0), axis=1).astype(jnp.bfloat16)
-    own = jnp.concatenate([normed, listed], axis=1).reshape(chunks, rows, width + pad)
+    listed = listed.reshape(chunks, rows, pad)
+    share = rows * 5 // 256 * 16
 
     bf16 = jnp.bfloat16
     dma = pltpu.SemaphoreType.DMA
     out = pl.pallas_call(
-        partial(layer_kernel, chunks, n_z, columns, width, rows_z),
+        partial(layer_kernel, chunks, n_z, columns, width, rows_z, share, 1),
         out_shape=jax.ShapeDtypeStruct((chunks, rows_z, width), bf16),
-        in_specs=[pl.BlockSpec(memory_space=pl.ANY)] * 7,
+        in_specs=[
+            pl.BlockSpec(memory_space=pl.ANY),
+            pl.BlockSpec(memory_space=pltpu.VMEM),
+            pl.BlockSpec(memory_space=pltpu.VMEM),
+        ]
+        + [pl.BlockSpec(memory_space=pl.ANY)] * 6,
         out_specs=pl.BlockSpec(memory_space=pltpu.VMEM),
         scratch_shapes=[
             pltpu.VMEM((4, chunks, 2, rows, width + pad), bf16),
@@ -365,14 +420,15 @@
             pltpu.VMEM((s_inner, width), bf16),
             pltpu.VMEM((2 * rows, columns * inner), bf16),
             pltpu.VMEM((4 * rows_z, s_inner), bf16),
+            pltpu.VMEM((chunks, n_z, rows_z, width), bf16),
             dma((6,)),
             dma((chunks,)),
             dma((chunks, 3)),
-            dma((chunks, 4)),
+            dma((chunks, 10)),
             dma((chunks, 4)),
             dma((chunks, 3)),
             dma((chunks, n_z)),
-            dma((chunks, 4, 2)),
+            dma((chunks, 4, 4)),
             dma((chunks, 4)),
             dma((chunks, 3)),
             dma((chunks, n_z)),
@@ -381,7 +437,9 @@
             collective_id=0, has_side_effects=True, vmem_limit_bytes=62 * 1024 * 1024
         ),
     )(
-        own,
+        tokens.reshape(n_z, 2, chunks, rows_z, width),
+        norm_gain.reshape(1, width),
+        listed,
         expert_gate,
         expert_up,
         expert_down.reshape(columns * inner, width),

time: 141 us -> 126 us (0.89)
  Pallas kernels: 131 us -> 117 us
  other arithmetic: 6.56 us -> 1.22 us
  local copies, waits for them, and re-layouts: 2.74 us -> 5.68 us
    pallas_call x1, Pallas kernels: 131 us -> 117 us  [on_device(): pl.pallas_call(partial(layer_kernel, chunks, n_z, columns, width, rows_z,...]
    convert_element_type x2 -> x0, other arithmetic: 3.13 us -> none  [the longest x1 1.77 us: rms_rows(): values = tokens.astype(jnp.float32)]
    concatenate x1 -> x0, other arithmetic: 2.49 us -> none  [on_device(): jnp.concatenate([normed, listed], axis=1).reshape(chunks, rows, width + pad)]
    reshape x3, local copies, waits for them, and re-layouts: 0.27 us -> 2.36 us  [half(): split = a.reshape((n_z, 2, chunks, rows_z) + a.shape[1:])]
where the time goes in v2:
time: 126 us; the launch traced here: 124 us
  Pallas kernels  117 us (93%)
  local copies, waits for them, and re-layouts  5.68 us (5%)
    pallas_call x1, Pallas kernels, on_device(): pl.pallas_call(partial(layer_kernel, chunks, n_z, columns, width, rows_z,...  117 us

profile of v2, /device:TPU:0, one launch (start us, length us, event | category | flops | bytes accessed | tf_op | source)
XLA Modules:
  0.0 124.2 jit_solution(1957021720771302078)
XLA Ops:
  0.0 0.8 reshape.62
  0.8 0.1 convert_element_type.46
  0.9 1.3 %reshape.59.gain_ref = f32[1,2560]{1,0:T(1,128)} reshape(f32[2560]{0:T(1024)} %param.15) | data formatting | bytes 20480 | tf_op jit(solution)/shard_map/reshape | solution.py:441
  2.2 0.8 reshape.61
  3.0 0.1 reshape.65
  3.1 0.8 reshape.60
  4.0 0.1 eq.17
  4.0 1.2 select_reduce_fusion
  5.2 117.2 %shard_map.109 = bf16[2,32,2560]{2,1,0:T(8,128)(2,1)} custom-call(bf16[4,2,2,32,2560]{4,3,2,1,0:T(8,128)(2,1)} %bitcast.29, f32[1,2560]{1,0:T(1,128)} %reshape.59.gain_ref, bf16[2,128,128]{2,1,0:T(8,128)(2,1)} %bitcast.31, bf16[2,384,2560]{2,1,0:T(8,128)(2,1)} %gate_hbm.1, bf16[2,384,2560]{2,1,0:T(8,128)(2,1)} %up_hbm.1, bf16[768,2560]{1,0:T(8,128)(2,1)} %bitcast.28, ...), custom_call_target="tpu_custom_call" | custom-call | tf_op jit(solution)/shard_map/pallas_call | solution.py:399
  122.5 1.7 %copy.31 = bf16[64,2560]{1,0:T(8,128)(2,1)} copy(bf16[64,2560]{1,0:T(8,128)(2,1)} %bitcast.30) | data formatting | bytes 655360
  (7 shorter events, 0.1 us)
